TPU v7x, 256 devices: a whole 4x4x8 slice. The times are simulated.
256 devices in a mesh: ctx: 2 (over core), exp: 8 (over z), tp: 16 (over y, x).
Axes of the slice: x: 4, y: 4, z: 8, core: 2. Of those that a mesh axis runs over, the one named last changes fastest.
Arguments:
- conv_in: bfloat16 [8, 256, 4096], P('exp', 'ctx', 'tp'), may hold values from -6 to 6
- gate_in: bfloat16 [8, 256, 4096], P('exp', 'ctx', 'tp'), may hold values from -6 to 6
- residual: bfloat16 [8, 256, 2048], P('exp', 'ctx'), may hold values from -6 to 6
- conv_weight: float32 [4, 4096], P(None, 'tp'), may hold values from -3 to 3
- conv_bias: float32 [4096], P('tp'), may hold values from -3 to 3
- proj_weight: bfloat16 [4096, 288], P('tp'), may hold values from -0.09375 to 0.09375
- step_weight: bfloat16 [256, 4096], P(None, 'tp'), may hold values from -0.375 to 0.375
- step_bias: float32 [4096], P('tp'), may hold values from -6 to -2
- decay_log: float32 [16, 4096], P(None, 'tp'), may hold values from -3 to 2
- skip_gain: float32 [4096], P('tp'), may hold values from 0.5 to 1.5
- out_weight: bfloat16 [4096, 2048], P('tp'), may hold values from -0.09375 to 0.09375
- norm_gain: float32 [2048], replicated, may hold values from 0.5 to 1.5
- expert_ids: int32 [8, 256, 2], P('exp', 'ctx'), may hold values from 0 to 7, all different within a row; in each aligned block of 128 rows (0 to 127, 128 to 255, ..., all dimensions but the last counted through in order) at most 64 rows name the same one
- route_gates: float32 [8, 256, 2], P('exp', 'ctx'), may hold values from 0.2 to 1
- expert_weight: bfloat16 [8, 3, 2048, 14336], P('exp', None, None, ('ctx', 'tp')), may hold values from -0.125 to 0.125
Outputs:
- layer_out: bfloat16 [8, 256, 2048], P('exp', 'ctx', 'tp')
Inputs may be any that keep to these rules, and one draw needn't show every extreme that they name: `expert_ids`: the 2 picks of a token differ. Among the picks of the 128 tokens of one sequence block, no expert is named more than 64 times, and in some block one expert is named exactly 64 times.
All inputs are finite; a program needn't handle non-finite values.
Results may differ from a plain program's by a relative error of at most 0.015.
Values may be sent and summed in bfloat16 or wider, within the bound.
A program may use at most 128 MiB of HBM per device.

v0:
```python
import math
import jax
import jax.numpy as jnp
from jax import lax
from jax.sharding import PartitionSpec as P

D = 2048
STATE = 16
DT_RANK = 256
TOP = 2
CAP = 64


def from_behind(block, axis, distance):
    devices = range(lax.axis_size(axis))
    route = [(i - distance, i) for i in devices if i - distance in devices]
    return lax.ppermute(block, axis, route)


def prefix(value, axis, join, neutral):
    count, mine = (lax.axis_size(axis), lax.axis_index(axis))
    pieces = jax.tree.map(lambda part: lax.all_gather(part, axis), value)
    running = jax.tree.map(
        lambda part, zero: jnp.full_like(part, 0) + jnp.asarray(zero, part.dtype), value, neutral
    )

    def hop(position, running):
        longer = join(running, jax.tree.map(lambda part: part[position], pieces))
        return jax.tree.map(lambda new, old: jnp.where(position < mine, new, old), longer, running)

    return lax.fori_loop(0, count - 1, hop, running)


def chain_pair(earlier, later):
    return (earlier[0] * later[0], later[0] * earlier[1] + later[1])


def body(
    conv_in,
    gate_in,
    residual,
    conv_weight,
    conv_bias,
    proj_weight,
    step_weight,
    step_bias,
    decay_log,
    skip_gain,
    out_weight,
    norm_gain,
    expert_ids,
    route_gates,
    expert_weight,
):
    highest = lax.Precision.HIGHEST
    local_x = conv_in[0]
    token_rows = local_x.shape[0]
    channels = local_x.shape[1]
    tap_count = conv_weight.shape[0]
    before = from_behind(local_x[token_rows - tap_count + 1 :], "ctx", 1)
    extended = jnp.concatenate([before, local_x], axis=0).astype(jnp.float32)
    convolved = conv_bias[None, :] + sum(
        (conv_weight[k][None, :] * extended[k : k + token_rows] for k in range(tap_count))
    )
    xconv = jax.nn.silu(convolved).astype(jnp.bfloat16)
    projected = lax.psum(jnp.dot(xconv, proj_weight, preferred_element_type=jnp.float32), "tp")
    rank_part = projected[:, :DT_RANK].astype(jnp.bfloat16)
    input_map = projected[:, DT_RANK : DT_RANK + STATE]
    output_map = projected[:, DT_RANK + STATE :]
    step_sizes = jax.nn.softplus(
        jnp.dot(rank_part, step_weight, preferred_element_type=jnp.float32) + step_bias
    )
    decay_rates = -jnp.exp(decay_log)
    xfloat = xconv.astype(jnp.float32)
    driven = step_sizes * xfloat
    span = math.gcd(token_rows, 16)
    block_total = token_rows // span

    def run_block(state, pieces):
        steps_here, driven_here, in_here, out_here = pieces
        emitted = []
        for inner_step in range(span):
            state = (
                jnp.exp(steps_here[inner_step][None, :] * decay_rates) * state
                + driven_here[inner_step][None, :] * in_here[inner_step][:, None]
            )
            emitted.append(jnp.sum(out_here[inner_step][:, None] * state, axis=0))
        return (state, jnp.stack(emitted))

    pieces = (
        step_sizes.reshape(block_total, span, channels),
        driven.reshape(block_total, span, channels),
        input_map.reshape(block_total, span, STATE),
        output_map.reshape(block_total, span, STATE),
    )
    last_state, local_out = lax.scan(run_block, jnp.zeros((STATE, channels), jnp.float32), pieces)
    local_out = local_out.reshape(token_rows, channels)
    elapsed = jnp.cumsum(step_sizes, axis=0)
    last_decay = jnp.exp(elapsed[token_rows - 1][None, :] * decay_rates)
    incoming = prefix(
        (last_decay, last_state),
        "ctx",
        chain_pair,
        (jnp.ones_like(last_decay), jnp.zeros_like(last_state)),
    )[1]
    carried = jnp.sum(
        output_map[:, :, None] * jnp.exp(elapsed[:, None, :] * decay_rates[None]) * incoming[None],
        axis=1,
    )
    scanned = local_out + carried + skip_gain * xfloat
    gated = (scanned * jax.nn.silu(gate_in[0].astype(jnp.float32))).astype(jnp.bfloat16)
    partial_out = jnp.dot(gated, out_weight, preferred_element_type=jnp.float32)
    quarter = D // lax.axis_size("tp")
    lane_start = lax.axis_index("tp") * quarter
    expert_count = lax.axis_size("exp")
    picks = expert_ids[0]
    onehot = (picks[:, :, None] == jnp.arange(expert_count, dtype=jnp.int32)).astype(jnp.int32)
    flat_hot = onehot.reshape(token_rows * TOP, expert_count)
    ranks = jnp.cumsum(flat_hot, axis=0) - 1
    within = jnp.sum(ranks * flat_hot, axis=1).reshape(token_rows, TOP)
    places = picks * CAP + within
    table = (places[:, :, None] == jnp.arange(expert_count * CAP, dtype=jnp.int32)).astype(
        jnp.float32
    )
    chooser = jnp.sum(table, axis=1).astype(jnp.bfloat16)
    blender = jnp.sum(table * route_gates[0][:, :, None], axis=1)
    mixed = lax.psum_scatter(partial_out, "tp", scatter_dimension=1, tiled=True)
    own_residual = lax.dynamic_slice_in_dim(residual[0], lane_start, quarter, 1)
    stream = (own_residual.astype(jnp.float32) + mixed).astype(jnp.bfloat16)
    sfloat = stream.astype(jnp.float32)
    squares = lax.psum(jnp.sum(sfloat * sfloat, axis=1), "tp")
    own_gain = lax.dynamic_slice_in_dim(norm_gain, lane_start, quarter, 0)
    normed = (sfloat * lax.rsqrt(squares[:, None] / D + 1e-06) * own_gain).astype(jnp.bfloat16)
    picked = lax.dot_general(
        chooser, normed, (((0,), (0,)), ((), ())), preferred_element_type=jnp.float32
    )
    arrived = lax.all_to_all(
        picked.astype(jnp.bfloat16).reshape(expert_count, CAP, normed.shape[1]),
        "exp",
        split_axis=0,
        concat_axis=0,
        tiled=True,
    )
    arrived = lax.all_gather(arrived, "tp", axis=2, tiled=True)
    slot_rows = arrived.reshape(-1, D)
    local_weights = expert_weight[0]
    piece = lax.all_gather(local_weights, "ctx", axis=2, tiled=True)
    gate_part = jnp.dot(slot_rows, piece[0], preferred_element_type=jnp.float32)
    up_part = jnp.dot(slot_rows, piece[1], preferred_element_type=jnp.float32)
    hidden = (jax.nn.silu(gate_part) * up_part).astype(jnp.bfloat16)
    summed = jnp.zeros((slot_rows.shape[0], D), jnp.float32) + lax.dot_general(
        hidden, piece[2], (((1,), (1,)), ((), ())), preferred_element_type=jnp.float32
    )
    expert_out = (
        lax.psum_scatter(summed, "tp", scatter_dimension=1, tiled=True)
        .astype(jnp.bfloat16)
        .reshape(expert_count, CAP, quarter)
    )
    returned = lax.all_to_all(expert_out, "exp", split_axis=0, concat_axis=0, tiled=True)
    moe = jnp.dot(
        blender,
        returned.reshape(expert_count * CAP, quarter).astype(jnp.float32),
        precision=highest,
        preferred_element_type=jnp.float32,
    )
    final = (sfloat + moe).astype(jnp.bfloat16)
    return final[None]


def solution(mesh):
    placed = (
        P("exp", "ctx", "tp"),
        P("exp", "ctx", "tp"),
        P("exp", "ctx", None),
        P(None, "tp"),
        P("tp"),
        P("tp", None),
        P(None, "tp"),
        P("tp"),
        P(None, "tp"),
        P("tp"),
        P("tp", None),
        P(),
        P("exp", "ctx", None),
        P("exp", "ctx", None),
        P("exp", None, None, ("ctx", "tp")),
    )
    return jax.shard_map(
        body, mesh=mesh, in_specs=placed, out_specs=P("exp", "ctx", "tp"), check_vma=False
    )
```

profile of v0, /device:TPU:2, one launch (start us, length us, event | category | flops | bytes accessed | tf_op | source)
XLA Modules:
  0.0 459.3 jit_solution(14481502077356869707)
XLA Ops:
  6.5 0.8 slice_bitcast_fusion.10
  7.3 1.7 collective-permute-start
  9.1 0.8 fusion.63
  9.9 0.9 maximum_convert_fusion
  10.8 0.8 multiply_convert_fusion.1
  11.6 1.8 fusion.64
  13.4 96.1 %all-reduce.2.cloned.1.call-done = f32[128,288]{0,1:T(8,128)} async-done(((f32[128,288]{0,1:T(8,128)}), f32[128,288]{0,1:T(8,128)}) %all-reduce.2.cloned.1.call-update) | async-done | bytes 147472 | tf_op jit(solution)/shard_map/psum | solution.py:66
  109.5 0.7 fusion.62
  110.4 1.2 convert_multiply_fusion.2
  111.7 0.2 reduce_window_sum.24
  111.9 8.2 %while.3 = (s32[]{:T(128)}, f32[16,256]{1,0:T(8,128)S(1)}, f32[8,16,256]{2,1,0:T(8,128)S(1)}, f32[8,16,256]{2,1,0:T(8,128)S(1)}, f32[16,256]{1,0:T(8,128)S(1)}, ...) while((s32[]{:T(128)}, f32[16,256]{1,0:T(8,128)S(1)}, ...), condition=%wide.region_18.19_spmd.clone, body=%wide.region_1.18_spmd.clone.sunk | while | flops 577554 | bytes 505064 | solution.py:96
  111.9 0.2 fusion.77
  112.1 0.2 constant_dynamic-slice_fusion.65
  112.3 0.2 multiply_reduce_fusion.22
  112.6 0.1 multiply_reduce_fusion.25
  113.0 0.2 fusion.77
  113.1 0.2 constant_dynamic-slice_fusion.65
  113.3 0.2 multiply_reduce_fusion.22
  113.6 0.1 multiply_reduce_fusion.25
  114.0 0.2 fusion.77
  114.2 0.2 constant_dynamic-slice_fusion.65
  114.4 0.2 multiply_reduce_fusion.22
  115.0 0.2 fusion.77
  115.2 0.2 constant_dynamic-slice_fusion.65
  115.4 0.2 multiply_reduce_fusion.22
  116.1 0.2 fusion.77
  116.2 0.2 constant_dynamic-slice_fusion.65
  116.4 0.2 multiply_reduce_fusion.22
  117.1 0.2 fusion.77
  117.3 0.2 constant_dynamic-slice_fusion.65
  117.4 0.2 multiply_reduce_fusion.22
  118.1 0.2 fusion.77
  118.3 0.2 constant_dynamic-slice_fusion.65
  118.5 0.2 multiply_reduce_fusion.22
  119.1 0.2 fusion.77
  119.3 0.2 constant_dynamic-slice_fusion.65
  119.5 0.2 multiply_reduce_fusion.22
  120.2 1.8 all-gather
  122.0 1.8 all-gather.1
  123.8 0.7 multiply_reduce_fusion.16
  124.6 0.1 fusion.41
  124.7 1.3 fusion.65
  126.1 0.1 copy.31
  126.2 0.1 eq.43
  126.4 0.1 eq.39
  126.5 0.6 reduce-window.6
  127.1 0.2 slice_reduce_fusion
  127.5 0.1 reshape.246
  127.7 0.8 dynamic_slice.31
  128.5 0.2 convert_reduce_fusion
  128.6 76.4 %reduce-scatter.3.cloned.1.call-done = f32[128,128]{1,0:T(8,128)} async-done(((f32[128,2048]{1,0:T(8,128)}), f32[128,128]{1,0:T(8,128)}) %reduce-scatter.3.cloned.1.call-update) | async-done | bytes 65552 | tf_op jit(solution)/shard_map/reduce_scatter | solution.py:127
  205.1 0.9 fusion.50
  206.0 36.3 %psum.15 = f32[128]{0:T(128)S(1)} all-reduce(f32[128]{0:T(128)S(1)} %get-tuple-element.158), channel_id=1, replica_groups=mesh['ctx'=2,'exp'=8,'tp'=16] {'tp'}, use_global_device_ids=true, to_apply=%region_28.29 | all-reduce | flops 128 | bytes 1024 | tf_op jit(solution)/shard_map/psum | solution.py:131
  242.3 0.3 convolution_convert_fusion
  242.6 16.0 %all_to_all.10 = bf16[8,64,128]{2,1,0:T(8,128)(2,1)} all-to-all(bf16[8,64,128]{2,1,0:T(8,128)(2,1)S(1)} %bitcast.278), channel_id=1, replica_groups=mesh['ctx'=2,'exp'=8,'tp'=16] {'exp'}, dimensions={0} | all-to-all | bytes 262144 | tf_op jit(solution)/shard_map/all_to_all | solution.py:137
  258.7 0.5 all-gather.8.cloned.1.call-update
  259.2 44.6 %all-gather.6.cloned.1.call-done = bf16[8,64,2048]{2,1,0:T(8,128)(2,1)} async-done(((bf16[8,64,128]{2,1,0:T(8,128)(2,1)}), bf16[8,64,2048]{2,1,0:T(8,128)(2,1)}) %all-gather.6.cloned.1.call-update) | async-done | bytes 2097168 | tf_op jit(solution)/shard_map/all_gather | solution.py:144
  303.8 29.3 %all-gather.8.cloned.1.call-done = bf16[1,3,2048,896]{2,3,1,0:T(8,128)(2,1)} async-done(((bf16[1,3,2048,448]{2,3,1,0:T(8,128)(2,1)}), bf16[1,3,2048,896]{2,3,1,0:T(8,128)(2,1)}) %all-gather.8.cloned.1.call-update) | async-done | bytes 11010064 | tf_op jit(solution)/shard_map/all_gather | solution.py:147
  333.1 6.3 %fusion.35 = f32[512,896]{1,0:T(8,128)} fusion(bf16[512,2048]{1,0:T(8,128)(2,1)} %bitcast.364, bf16[1,3,2048,896]{2,3,1,0:T(8,128)(2,1)} %all-gather.8.cloned.1.call-done), kind=kOutput, calls=%fused_computation.135 | convolution fusion | flops 1879048192 | bytes 7602176 | tf_op jit(solution)/shard_map/dot_general | solution.py:148
  339.4 10.9 %fusion.33 = f32[512,2048]{1,0:T(8,128)} fusion(bf16[1,3,2048,896]{2,3,1,0:T(8,128)(2,1)} %all-gather.8.cloned.1.call-done, f32[512,896]{1,0:T(8,128)} %fusion.35, bf16[512,2048]{1,0:T(8,128)(2,1)} %bitcast.365), kind=kOutput, calls=%fused_computation.131 | convolution fusion | flops 3760848896 | bytes 15466496 | tf_op jit(solution)/shard_map/dot_general | solution.py:151
  350.4 84.7 %reduce-scatter.5.cloned.1.call-done = f32[512,128]{1,0:T(8,128)} async-done(((f32[512,2048]{1,0:T(8,128)}), f32[512,128]{1,0:T(8,128)}) %reduce-scatter.5.cloned.1.call-update) | async-done | bytes 262160 | tf_op jit(solution)/shard_map/reduce_scatter | solution.py:155
  435.1 1.0 convert_element_type.75
  436.0 15.9 %all_to_all.11 = bf16[8,64,128]{2,1,0:T(8,128)(2,1)S(1)} all-to-all(bf16[8,64,128]{2,1,0:T(8,128)(2,1)S(1)} %bitcast.277), channel_id=1, replica_groups=mesh['ctx'=2,'exp'=8,'tp'=16] {'exp'}, dimensions={0} | all-to-all | bytes 262144 | tf_op jit(solution)/shard_map/all_to_all | solution.py:159
  451.9 0.9 fusion.37
  (92 shorter events, 4.3 us)
Async XLA Ops:
  6.5 118.2 %copy-start = (bf16[256,2048]{1,0:T(8,128)(2,1)S(1)}, bf16[256,2048]{1,0:T(8,128)(2,1)}, u32[]{:S(2)}) copy-start(bf16[256,2048]{1,0:T(8,128)(2,1)} %param.27) | copy-start | bytes 3145732
  6.5 105.3 %copy-start.2 = (f32[16,256]{1,0:T(8,128)S(1)}, f32[16,256]{1,0:T(8,128)}, u32[]{:S(2)}) copy-start(f32[16,256]{1,0:T(8,128)} %param.25) | copy-start | bytes 49156
  6.5 103.0 %all-reduce.2.cloned.1.call-start = ((), (), s32[]{:S(2)}) async-start(), calls=%async_computation.4 | async-start | bytes 294912 | tf_op jit(solution)/shard_map/psum | solution.py:66
  7.3 2.6 collective-permute-start
  13.3 191.7 %reduce-scatter.3.cloned.1.call-start = ((), (), s32[]{:S(2)}) async-start(), calls=%async_computation.5 | async-start | bytes 1114112 | tf_op jit(solution)/shard_map/reduce_scatter | solution.py:127
  111.9 12.7 %copy-start.1 = (bf16[1,128,256]{2,1,0:T(8,128)(2,1)S(1)}, bf16[1,128,256]{2,1,0:T(8,128)(2,1)}, u32[]{:S(2)}) copy-start(bf16[1,128,256]{2,1,0:T(8,128)(2,1)} %param.18) | copy-start | bytes 196612
  111.9 12.6 %copy-start.3 = (f32[256]{0:T(256)S(1)}, f32[256]{0:T(256)}, u32[]{:S(2)}) copy-start(f32[256]{0:T(256)} %param.21) | copy-start | bytes 3076
  111.9 12.6 %copy-start.4 = (f32[256]{0:T(256)S(1)}, f32[256]{0:T(256)}, u32[]{:S(2)}) copy-start(f32[256]{0:T(256)} %param.26) | copy-start | bytes 3076
  124.5 1.6 copy-start.5
  124.7 3.8 copy-start.6
  126.1 177.8 %all-gather.6.cloned.1.call-start = ((), (), s32[]{:S(2)}) async-start(), calls=%async_computation.6 | async-start | bytes 2228224 | tf_op jit(solution)/shard_map/all_gather | solution.py:144
  258.6 74.5 %all-gather.8.cloned.1.call-start = ((), (), s32[]{:S(2)}) async-start(), calls=%async_computation.8 | async-start | bytes 16515072 | tf_op jit(solution)/shard_map/all_gather | solution.py:147
  259.2 175.9 %reduce-scatter.5.cloned.1.call-start = ((), (), s32[]{:S(2)}) async-start(), calls=%async_computation.7 | async-start | bytes 4456448 | tf_op jit(solution)/shard_map/reduce_scatter | solution.py:155
Sparse Core Ops, SparseCore 0:
  13.5 95.9 all-reduce.1
  126.2 78.8 reduce-scatter.2
  258.7 45.0 all-gather.5
  305.5 27.5 all-gather.7
  350.5 84.5 reduce-scatter.4
where the time goes:
time: 460 us; the launch traced here: 459 us
  waiting for transfers between devices  332 us (72%)
  blocking collectives  71.8 us (16%)
  matrix products  22.6 us (5%)
  between operations  13.4 us (3%)
  other arithmetic  10 us (2%)
  local copies, waits for them, and re-layouts  7.51 us (2%)
    psum x1, waiting for transfers between devices, body(): lax.psum(jnp.dot(xconv, proj_weight, preferred_element_type=jnp.float32),...  96.1 us
    reduce_scatter x1, waiting for transfers between devices, body(): lax.psum_scatter(summed, 'tp', scatter_dimension=1, tiled=True)  84.7 us
    reduce_scatter x1, waiting for transfers between devices, body(): mixed = lax.psum_scatter(partial_out, 'tp', scatter_dimension=1, tiled=True)  76.4 us
    all_gather x1, waiting for transfers between devices, body(): arrived = lax.all_gather(arrived, 'tp', axis=2, tiled=True)  44.6 us
    psum x1, blocking collectives, body(): squares = lax.psum(jnp.sum(sfloat * sfloat, axis=1), 'tp')  36.3 us
    all_gather x1, waiting for transfers between devices, body(): piece = lax.all_gather(local_weights, 'ctx', axis=2, tiled=True)  29.3 us
    all_to_all x1, blocking collectives, body(): lax.all_to_all(picked.astype(jnp.bfloat16).reshape(expert_count, CAP, nor...  16 us
    all_to_all x1, blocking collectives, body(): lax.all_to_all(expert_out, 'exp', split_axis=0, concat_axis=0, tiled=True)  15.9 us
  transfers between devices with their start and end apart: 6, of which 5 were waited for; matrix products, arithmetic and copies ran while one was open for 1% of the time, Pallas kernels for 0%

commit v1 on v0

--- a/solution.py
+++ b/solution.py
@@ -63,7 +63,10 @@
         (conv_weight[k][None, :] * extended[k : k + token_rows] for k in range(tap_count))
     )
     xconv = jax.nn.silu(convolved).astype(jnp.bfloat16)
-    projected = lax.psum(jnp.dot(xconv, proj_weight, preferred_element_type=jnp.float32), "tp")
+    projected = jnp.sum(
+        lax.all_gather(jnp.dot(xconv, proj_weight, preferred_element_type=jnp.float32), "tp"),
+        axis=0,
+    )
     rank_part = projected[:, :DT_RANK].astype(jnp.bfloat16)
     input_map = projected[:, DT_RANK : DT_RANK + STATE]
     output_map = projected[:, DT_RANK + STATE :]

time: 460 us -> 420 us (0.913)
  waiting for transfers between devices: 332 us -> 291 us
    psum x1 -> x0, waiting for transfers between devices: 96.1 us -> none  [body(): lax.psum(jnp.dot(xconv, proj_weight, preferred_element_type=jnp.float32),...]
    all_gather x0 -> x1, waiting for transfers between devices: none -> 55.9 us  [body(): lax.all_gather(jnp.dot(xconv, proj_weight, preferred_element_type=jnp.flo...]
where the time goes in v1:
time: 420 us
  waiting for transfers between devices  291 us (69%)
  blocking collectives  71.8 us (17%)
  matrix products  21.7 us (5%)
  between operations  13.4 us (3%)
  other arithmetic  10.4 us (2%)
  local copies, waits for them, and re-layouts  9.17 us (2%)
    reduce_scatter x1, waiting for transfers between devices, body(): lax.psum_scatter(summed, 'tp', scatter_dimension=1, tiled=True)  84.6 us
    reduce_scatter x1, waiting for transfers between devices, body(): mixed = lax.psum_scatter(partial_out, 'tp', scatter_dimension=1, tiled=True)  76 us
    all_gather x1, waiting for transfers between devices, body(): lax.all_gather(jnp.dot(xconv, proj_weight, preferred_element_type=jnp.flo...  55.9 us
    all_gather x1, waiting for transfers between devices, body(): arrived = lax.all_gather(arrived, 'tp', axis=2, tiled=True)  44.6 us
    psum x1, blocking collectives, body(): squares = lax.psum(jnp.sum(sfloat * sfloat, axis=1), 'tp')  36.3 us
    all_gather x1, waiting for transfers between devices, body(): piece = lax.all_gather(local_weights, 'ctx', axis=2, tiled=True)  29.3 us
    all_to_all x1, blocking collectives, body(): lax.all_to_all(picked.astype(jnp.bfloat16).reshape(expert_count, CAP, nor...  16 us
    all_to_all x1, blocking collectives, body(): lax.all_to_all(expert_out, 'exp', split_axis=0, concat_axis=0, tiled=True)  15.9 us
  transfers between devices with their start and end apart: 6, of which 5 were waited for; matrix products, arithmetic and copies ran while one was open for 1% of the time, Pallas kernels for 0%

profile of v1, /device:TPU:2, one launch (start us, length us, event | category | flops | bytes accessed | tf_op | source)
XLA Modules:
  0.0 419.8 jit_solution(8504531070430706783)
XLA Ops:
  6.5 0.8 slice_bitcast_fusion.10
  7.3 1.7 collective-permute-start
  9.1 0.8 fusion.63
  9.9 0.9 maximum_convert_fusion
  10.8 0.8 multiply_convert_fusion.1
  11.5 1.8 fusion.64
  13.4 55.9 %all-gather.10.cloned.1.call-done = f32[2048,288]{0,1:T(8,128)} async-done(((f32[128,288]{0,1:T(8,128)}), f32[2048,288]{0,1:T(8,128)}) %all-gather.10.cloned.1.call-update) | async-done | bytes 2359312 | tf_op jit(solution)/shard_map/all_gather | solution.py:67
  69.3 2.1 copy.38
  71.4 0.4 bitcast_reduce_fusion
  72.0 0.3 copy-done.1
  72.3 0.3 convert_multiply_fusion.2
  72.6 0.2 reduce_window_sum.24
  72.8 8.2 %while.3 = (s32[]{:T(128)}, f32[16,256]{1,0:T(8,128)S(1)}, f32[8,16,256]{2,1,0:T(8,128)S(1)}, f32[8,16,256]{2,1,0:T(8,128)S(1)}, f32[16,256]{1,0:T(8,128)S(1)}, ...) while((s32[]{:T(128)}, f32[16,256]{1,0:T(8,128)S(1)}, ...), condition=%wide.region_18.19_spmd.clone, body=%wide.region_1.18_spmd.clone.sunk | while | flops 577554 | bytes 505064 | solution.py:99
  72.8 0.2 fusion.77
  73.0 0.2 constant_dynamic-slice_fusion.65
  73.2 0.2 multiply_reduce_fusion.22
  73.9 0.2 fusion.77
  74.0 0.2 constant_dynamic-slice_fusion.65
  74.2 0.2 multiply_reduce_fusion.22
  74.9 0.2 fusion.77
  75.1 0.2 constant_dynamic-slice_fusion.65
  75.3 0.2 multiply_reduce_fusion.22
  75.9 0.2 fusion.77
  76.1 0.2 constant_dynamic-slice_fusion.65
  76.3 0.2 multiply_reduce_fusion.22
  77.0 0.2 fusion.77
  77.1 0.2 constant_dynamic-slice_fusion.65
  77.3 0.2 multiply_reduce_fusion.22
  78.0 0.2 fusion.77
  78.2 0.2 constant_dynamic-slice_fusion.65
  78.3 0.2 multiply_reduce_fusion.22
  79.0 0.2 fusion.77
  79.2 0.2 constant_dynamic-slice_fusion.65
  79.4 0.2 multiply_reduce_fusion.22
  80.0 0.2 fusion.77
  80.2 0.2 constant_dynamic-slice_fusion.65
  80.4 0.2 multiply_reduce_fusion.22
  81.1 1.8 all-gather.1
  82.9 1.8 all-gather.2
  84.7 0.7 multiply_reduce_fusion.16
  85.5 0.1 fusion.41
  85.6 1.3 fusion.65
  87.0 0.1 copy.32
  87.1 0.1 eq.43
  87.3 0.1 eq.39
  87.4 0.6 reduce-window.6
  88.0 0.2 slice_reduce_fusion
  88.4 0.1 reshape.246
  88.6 0.8 dynamic_slice.31
  89.4 0.2 convert_reduce_fusion
  89.5 76.0 %reduce-scatter.3.cloned.1.call-done = f32[128,128]{1,0:T(8,128)} async-done(((f32[128,2048]{1,0:T(8,128)}), f32[128,128]{1,0:T(8,128)}) %reduce-scatter.3.cloned.1.call-update) | async-done | bytes 65552 | tf_op jit(solution)/shard_map/reduce_scatter | solution.py:130
  165.6 0.9 fusion.50
  166.5 36.3 %psum.7 = f32[128]{0:T(128)S(1)} all-reduce(f32[128]{0:T(128)S(1)} %get-tuple-element.150), channel_id=1, replica_groups=mesh['ctx'=2,'exp'=8,'tp'=16] {'tp'}, use_global_device_ids=true, to_apply=%region_28.29 | all-reduce | flops 128 | bytes 1024 | tf_op jit(solution)/shard_map/psum | solution.py:134
  202.8 0.3 convolution_convert_fusion
  203.1 16.0 %all_to_all.10 = bf16[8,64,128]{2,1,0:T(8,128)(2,1)} all-to-all(bf16[8,64,128]{2,1,0:T(8,128)(2,1)S(1)} %bitcast.284), channel_id=1, replica_groups=mesh['ctx'=2,'exp'=8,'tp'=16] {'exp'}, dimensions={0} | all-to-all | bytes 262144 | tf_op jit(solution)/shard_map/all_to_all | solution.py:140
  219.1 0.5 all-gather.12.cloned.1.call-update
  219.7 44.6 %all-gather.8.cloned.1.call-done = bf16[8,64,2048]{2,1,0:T(8,128)(2,1)} async-done(((bf16[8,64,128]{2,1,0:T(8,128)(2,1)}), bf16[8,64,2048]{2,1,0:T(8,128)(2,1)}) %all-gather.8.cloned.1.call-update) | async-done | bytes 2097168 | tf_op jit(solution)/shard_map/all_gather | solution.py:147
  264.3 29.3 %all-gather.12.cloned.1.call-done = bf16[1,3,2048,896]{2,3,1,0:T(8,128)(2,1)} async-done(((bf16[1,3,2048,448]{2,3,1,0:T(8,128)(2,1)}), bf16[1,3,2048,896]{2,3,1,0:T(8,128)(2,1)}) %all-gather.12.cloned.1.call-update) | async-done | bytes 11010064 | tf_op jit(solution)/shard_map/all_gather | solution.py:150
  293.6 6.3 %fusion.35 = f32[512,896]{1,0:T(8,128)} fusion(bf16[512,2048]{1,0:T(8,128)(2,1)} %bitcast.370, bf16[1,3,2048,896]{2,3,1,0:T(8,128)(2,1)} %all-gather.12.cloned.1.call-done), kind=kOutput, calls=%fused_computation.135 | convolution fusion | flops 1879048192 | bytes 7602176 | tf_op jit(solution)/shard_map/dot_general | solution.py:151
  299.9 10.9 %fusion.33 = f32[512,2048]{1,0:T(8,128)} fusion(bf16[1,3,2048,896]{2,3,1,0:T(8,128)(2,1)} %all-gather.12.cloned.1.call-done, f32[512,896]{1,0:T(8,128)} %fusion.35, bf16[512,2048]{1,0:T(8,128)(2,1)} %bitcast.371), kind=kOutput, calls=%fused_computation.131 | convolution fusion | flops 3760848896 | bytes 15466496 | tf_op jit(solution)/shard_map/dot_general | solution.py:154
  310.9 84.6 %reduce-scatter.5.cloned.1.call-done = f32[512,128]{1,0:T(8,128)} async-done(((f32[512,2048]{1,0:T(8,128)}), f32[512,128]{1,0:T(8,128)}) %reduce-scatter.5.cloned.1.call-update) | async-done | bytes 262160 | tf_op jit(solution)/shard_map/reduce_scatter | solution.py:158
  395.5 1.0 convert_element_type.75
  396.5 15.9 %all_to_all.11 = bf16[8,64,128]{2,1,0:T(8,128)(2,1)S(1)} all-to-all(bf16[8,64,128]{2,1,0:T(8,128)(2,1)S(1)} %bitcast.283), channel_id=1, replica_groups=mesh['ctx'=2,'exp'=8,'tp'=16] {'exp'}, dimensions={0} | all-to-all | bytes 262144 | tf_op jit(solution)/shard_map/all_to_all | solution.py:162
  412.4 0.9 fusion.37
  (98 shorter events, 4.5 us)
Async XLA Ops:
  6.5 79.1 %copy-start = (bf16[256,2048]{1,0:T(8,128)(2,1)S(1)}, bf16[256,2048]{1,0:T(8,128)(2,1)}, u32[]{:S(2)}) copy-start(bf16[256,2048]{1,0:T(8,128)(2,1)} %param.27) | copy-start | bytes 3145732
  6.5 62.7 %all-gather.10.cloned.1.call-start = ((), (), s32[]{:S(2)}) async-start(), calls=%async_computation.7 | async-start | bytes 2506752 | tf_op jit(solution)/shard_map/all_gather | solution.py:67
  7.3 2.6 collective-permute-start
  13.3 152.3 %reduce-scatter.3.cloned.1.call-start = ((), (), s32[]{:S(2)}) async-start(), calls=%async_computation.4 | async-start | bytes 1114112 | tf_op jit(solution)/shard_map/reduce_scatter | solution.py:130
  71.4 0.9 copy-start.1
  71.4 0.9 copy-start.5
  71.4 1.4 copy-start.3
  72.8 12.6 %copy-start.2 = (bf16[1,128,256]{2,1,0:T(8,128)(2,1)S(1)}, bf16[1,128,256]{2,1,0:T(8,128)(2,1)}, u32[]{:S(2)}) copy-start(bf16[1,128,256]{2,1,0:T(8,128)(2,1)} %param.18) | copy-start | bytes 196612
  72.8 12.6 %copy-start.4 = (f32[256]{0:T(256)S(1)}, f32[256]{0:T(256)}, u32[]{:S(2)}) copy-start(f32[256]{0:T(256)} %param.21) | copy-start | bytes 3076
  72.8 12.6 %copy-start.6 = (f32[256]{0:T(256)S(1)}, f32[256]{0:T(256)}, u32[]{:S(2)}) copy-start(f32[256]{0:T(256)} %param.26) | copy-start | bytes 3076
  85.4 1.6 copy-start.7
  85.6 3.8 copy-start.8
  87.0 177.4 %all-gather.8.cloned.1.call-start = ((), (), s32[]{:S(2)}) async-start(), calls=%async_computation.5 | async-start | bytes 2228224 | tf_op jit(solution)/shard_map/all_gather | solution.py:147
  219.1 74.5 %all-gather.12.cloned.1.call-start = ((), (), s32[]{:S(2)}) async-start(), calls=%async_computation.8 | async-start | bytes 16515072 | tf_op jit(solution)/shard_map/all_gather | solution.py:150
  219.7 175.9 %reduce-scatter.5.cloned.1.call-start = ((), (), s32[]{:S(2)}) async-start(), calls=%async_computation.6 | async-start | bytes 4456448 | tf_op jit(solution)/shard_map/reduce_scatter | solution.py:158
Sparse Core Ops, SparseCore 0:
  13.5 55.7 all-gather.9
  87.1 78.4 reduce-scatter.2
  219.2 45.0 all-gather.7
  266.0 27.5 all-gather.11
  311.0 84.4 reduce-scatter.4
